TPU v7x, 256 devices: a whole 4x4x8 slice. The times are simulated.
256 devices in a mesh: row: 32 (over z, y_lo, core), col: 8 (over y_hi, x).
Axes of the slice: x: 4, y: 4 (y_hi: 2, y_lo: 2; y = y_hi * 2 + y_lo), z: 8, core: 2. Of those that a mesh axis runs over, the one named last changes fastest.
Arguments:
- matrix: float32 [14336, 14336], P('row', 'col'), may hold values from -16 to 16, as said below
- panels: float32 [2, 14336, 128], P(None, 'row'), may hold values from -0.050111484 to 0.050111484
- factors: float32 [2, 128, 128], replicated, may hold values from -1.2 to 1.6, as said below
Outputs:
- updated: float32 [14336, 14336], P('row', 'col')
Inputs may be any that keep to these rules, and one draw needn't show every extreme that they name: symmetric: matrix[r, c] equals matrix[c, r]. Each factors[p] is upper triangular, with diagonal entries between 0.8 and 1.6.
All inputs are finite; a program needn't handle non-finite values.
Results may differ from a plain program's by a relative error of at most 0.0001.
Values sent between devices are 32-bit elements; how exact they have to be, the bound alone decides.
A program may use at most 64 MiB of HBM per device.

v0:
```python
import jax
import jax.numpy as jnp
from jax import lax
from jax.sharding import PartitionSpec as P


def matmul(former, latter):
    return jnp.dot(former, latter, precision=lax.Precision.HIGHEST)


def transposed_dot(former, latter):
    return lax.dot_general(
        former, latter, (((0,), (0,)), ((), ())), precision=lax.Precision.HIGHEST
    )


def outer_drop(current, former, latter):
    return current - lax.dot_general(
        former, latter, (((1,), (1,)), ((), ())), precision=lax.Precision.HIGHEST
    )


def weights(forward, vectors, factor, correct):
    return matmul(forward, factor) - 0.5 * matmul(vectors, correct)


def row_sums(current, vector_rows, extra_terms):
    summed = lax.psum((transposed_dot(current, vector_rows),) + extra_terms, "row")
    return (summed[0], tuple(summed[1:]))


def shards(matrix, panels, factors):
    col_index = lax.axis_index("col")
    local_cols = matrix.shape[1]
    gathered = lax.all_gather(panels, "row", axis=1, tiled=True)
    vector_cols = lax.dynamic_slice_in_dim(gathered, col_index * local_cols, local_cols, 1)
    current = matrix
    for number in range(panels.shape[0]):
        vector_rows = panels[number]
        vcol_now = vector_cols[number]
        factor = factors[number]
        forward = lax.psum(matmul(current, vcol_now), "col")
        forward_cols, summed = row_sums(
            current, vector_rows, (transposed_dot(vector_rows, forward),)
        )
        correct = matmul(factor.T, matmul(summed[0], factor))
        wrow_now = weights(forward, vector_rows, factor, correct)
        wcol_now = weights(forward_cols, vcol_now, factor, correct)
        current = outer_drop(
            current,
            jnp.concatenate([vector_rows, wrow_now], axis=1),
            jnp.concatenate([wcol_now, vcol_now], axis=1),
        )
    return current


def solution(mesh):
    placed = (P("row", "col"), P(None, "row", None), P())
    return jax.shard_map(
        shards, mesh=mesh, in_specs=placed, out_specs=P("row", "col"), check_vma=False
    )
```

profile of v0, /device:TPU:1, one launch (start us, length us, event | category | flops | bytes accessed | tf_op | source)
XLA Modules:
  0.0 775.0 jit_solution(1958344349460214117)
XLA Ops:
  7.3 95.2 %all-gather.2.cloned.1.call-done = f32[2,14336,128]{2,1,0:T(8,128)} async-done(((f32[2,448,128]{2,1,0:T(8,128)}), f32[2,14336,128]{2,1,0:T(8,128)}) %all-gather.2.cloned.1.call-update) | async-done | bytes 14680080 | tf_op jit(solution)/shard_map/all_gather | solution.py:35
  102.5 2.5 dynamic-slice_bitcast_fusion
  105.0 0.9 copy-done.3
  105.9 3.4 convolution_bitcast_fusion
  109.4 7.8 %fusion.44 = f32[1792,128]{1,0:T(8,128)} fusion(f32[448,1792]{1,0:T(8,128)S(1)} %copy-done, f32[2,448,128]{2,1,0:T(8,128)} %param.4), kind=kOutput, calls=%fused_computation.57 | convolution fusion | flops 1233125376 | bytes 4358144 | tf_op jit(solution)/shard_map/dot_general | solution.py:12
  117.2 74.7 %all-reduce.7.cloned.1.call-done = f32[448,128]{1,0:T(8,128)} async-done(((f32[448,128]{1,0:T(8,128)}), f32[448,128]{1,0:T(8,128)}) %all-reduce.7.cloned.1.call-update) | async-done | bytes 229392 | tf_op jit(solution)/shard_map/psum | solution.py:42
  191.9 2.3 convolution_bitcast_fusion.2
  194.4 1.9 slice_bitcast_fusion
  196.3 1.3 fusion.32
  197.6 228.8 %all-reduce.13.cloned.1.call-done = (f32[1792,128]{1,0:T(8,128)}, f32[128,128]{0,1:T(8,128)}) async-done(((f32[1792,128]{1,0:T(8,128)}, f32[128,128]{0,1:T(8,128)}), (f32[1792,128]{1,0:T(8,128)}, f32[128,128]{0,1:T(8,128)})) %all-reduce.13.cloned.1.call-update) | async-done | bytes 983056 | tf_op jit(solution)/shard_map/psum | solution.py:28
  426.3 2.1 fusion.26
  428.4 1.1 fusion.30
  429.9 0.9 fusion.1
  431.2 5.1 convolution_subtract_fusion.1
  436.3 3.4 fusion.46
  439.9 7.8 %fusion.45 = f32[1792,128]{1,0:T(8,128)} fusion(f32[448,1792]{1,0:T(8,128)S(1)} %convolution_subtract_fusion.1, f32[2,448,128]{2,1,0:T(8,128)} %param.4), kind=kOutput, calls=%fused_computation.58 | convolution fusion | flops 1233125376 | bytes 4358144 | tf_op jit(solution)/shard_map/dot_general | solution.py:12
  447.7 75.9 %all-reduce.9.cloned.1.call-done = f32[448,128]{1,0:T(8,128)} async-done(((f32[448,128]{1,0:T(8,128)}), f32[448,128]{1,0:T(8,128)}) %all-reduce.9.cloned.1.call-update) | async-done | bytes 229392 | tf_op jit(solution)/shard_map/psum | solution.py:42
  523.6 2.3 convolution_bitcast_fusion.1
  525.9 2.0 fusion.24
  527.9 230.0 %all-reduce.11.cloned.1.call-done = (f32[1792,128]{1,0:T(8,128)}, f32[128,128]{0,1:T(8,128)}) async-done(((f32[1792,128]{1,0:T(8,128)}, f32[128,128]{0,1:T(8,128)}), (f32[1792,128]{1,0:T(8,128)}, f32[128,128]{0,1:T(8,128)})) %all-reduce.11.cloned.1.call-update) | async-done | bytes 983056 | tf_op jit(solution)/shard_map/psum | solution.py:28
  757.9 2.2 fusion.18
  760.1 1.1 fusion.22
  761.5 2.1 fusion
  764.0 4.5 convolution_subtract_fusion
  (35 shorter events, 2.7 us)
Async XLA Ops:
  6.5 99.4 %copy-start = (f32[448,1792]{1,0:T(8,128)S(1)}, f32[448,1792]{1,0:T(8,128)}, u32[]{:S(2)}) copy-start(f32[448,1792]{1,0:T(8,128)} %param.3) | copy-start | bytes 9633796
  6.5 96.0 %all-gather.2.cloned.1.call-start = ((), (), s32[]{:S(2)}) async-start(), calls=%async_computation | async-start | bytes 15138816 | tf_op jit(solution)/shard_map/all_gather | solution.py:35
  7.3 184.6 %all-reduce.7.cloned.1.call-start = ((), (), s32[]{:S(2)}) async-start(), calls=%async_computation.1 | async-start | bytes 458752 | tf_op jit(solution)/shard_map/psum | solution.py:42
  105.0 0.9 copy-start.3
  109.3 87.0 %copy-start.7 = (f32[2,128,128]{2,1,0:T(8,128)S(1)}, f32[2,128,128]{2,1,0:T(8,128)}, u32[]{:S(2)}) copy-start(f32[2,128,128]{2,1,0:T(8,128)} %param.5) | copy-start | bytes 393220
  109.3 317.0 %all-reduce.13.cloned.1.call-start = ((), (), s32[]{:S(2)}) async-start(), calls=%async_computation.4 | async-start | bytes 1966080 | tf_op jit(solution)/shard_map/psum | solution.py:28
  117.2 312.7 %copy-start.4 = (f32[1792,128]{1,0:T(8,128)S(1)}, f32[1792,128]{1,0:T(8,128)}, u32[]{:S(2)}) copy-start(f32[1792,128]{1,0:T(8,128)} %copy-done.3) | copy-start | bytes 2752516
  194.2 236.6 %copy-start.5 = (f32[2,448,128]{2,1,0:T(8,128)S(1)}, f32[2,448,128]{2,1,0:T(8,128)}, u32[]{:S(2)}) copy-start(f32[2,448,128]{2,1,0:T(8,128)} %param.4) | copy-start | bytes 1376260
  194.2 329.4 %all-reduce.9.cloned.1.call-start = ((), (), s32[]{:S(2)}) async-start(), calls=%async_computation.2 | async-start | bytes 458752 | tf_op jit(solution)/shard_map/psum | solution.py:42
  426.3 4.8 copy-start.9
  431.2 5.1 copy-start.1
  439.7 318.2 %all-reduce.11.cloned.1.call-start = ((), (), s32[]{:S(2)}) async-start(), calls=%async_computation.3 | async-start | bytes 1966080 | tf_op jit(solution)/shard_map/psum | solution.py:28
  757.9 5.7 copy-start.6
  757.9 5.7 copy-start.10
  757.9 6.1 copy-start.2
  757.9 6.1 copy-start.8
Sparse Core Ops, SparseCore 0:
  9.1 93.3 all-gather.1
  109.4 82.4 all-reduce.6
  194.6 231.7 all-reduce.12
  439.8 83.7 all-reduce.8
  526.2 231.7 all-reduce.10
where the time goes:
time: 775 us
  waiting for transfers between devices  705 us (91%)
  matrix products  50.4 us (7%)
  between operations  13.3 us (2%)
    psum x2, waiting for transfers between devices, row_sums(): lax.psum((transposed_dot(current, vector_rows),) + extra_terms, 'row')  459 us
    psum x2, waiting for transfers between devices, shards(): forward = lax.psum(matmul(current, vcol_now), 'col')  151 us
    all_gather x1, waiting for transfers between devices, shards(): gathered = lax.all_gather(panels, 'row', axis=1, tiled=True)  95.2 us
    dot_general x14, matrix products, matmul(): return jnp.dot(former, latter, precision=lax.Precision.HIGHEST)  20.8 us
    dot_general x4, matrix products, transposed_dot(): lax.dot_general(former, latter, (((0,), (0,)), ((), ())), precision=lax.P...  20.1 us
  transfers between devices with their start and end apart: 5, of which 5 were waited for; matrix products, arithmetic and copies ran while one was open for 3% of the time, Pallas kernels for 0%

commit v1 on v0

--- a/solution.py
+++ b/solution.py
@@ -2,6 +2,11 @@
 import jax.numpy as jnp
 from jax import lax
 from jax.sharding import PartitionSpec as P
+
+
+def gathered_along(x, mesh_axis, d):
+    shards = lax.all_gather(x, mesh_axis)
+    return jnp.concatenate(shards, axis=d)
 
 
 def matmul(former, latter):
@@ -32,7 +37,7 @@
 def shards(matrix, panels, factors):
     col_index = lax.axis_index("col")
     local_cols = matrix.shape[1]
-    gathered = lax.all_gather(panels, "row", axis=1, tiled=True)
+    gathered = gathered_along(panels, "row", 1)
     vector_cols = lax.dynamic_slice_in_dim(gathered, col_index * local_cols, local_cols, 1)
     current = matrix
     for number in range(panels.shape[0]):

time: 775 us -> 788 us (1.017)
  local copies, waits for them, and re-layouts: 5.37 us -> 22.4 us
    reshape x0 -> x1, local copies, waits for them, and re-layouts: none -> 12.1 us  [gathered_along(): return jnp.concatenate(shards, axis=d)]
where the time goes in v1:
time: 788 us; the launch traced here: 787 us
  waiting for transfers between devices  702 us (89%)
  matrix products  49.6 us (6%)
  local copies, waits for them, and re-layouts  22.4 us (3%)
  between operations  13.3 us (2%)
    psum x2, waiting for transfers between devices, row_sums(): lax.psum((transposed_dot(current, vector_rows),) + extra_terms, 'row')  455 us
    psum x2, waiting for transfers between devices, shards(): forward = lax.psum(matmul(current, vcol_now), 'col')  151 us
    all_gather x1, waiting for transfers between devices, gathered_along(): shards = lax.all_gather(x, mesh_axis)  95.2 us
    dot_general x4, matrix products, transposed_dot(): lax.dot_general(former, latter, (((0,), (0,)), ((), ())), precision=lax.P...  20.2 us
    dot_general x14, matrix products, matmul(): return jnp.dot(former, latter, precision=lax.Precision.HIGHEST)  20.1 us
  transfers between devices with their start and end apart: 5, of which 5 were waited for; matrix products, arithmetic and copies ran while one was open for 3% of the time, Pallas kernels for 0%

profile of v1, /device:TPU:1, one launch (start us, length us, event | category | flops | bytes accessed | tf_op | source)
XLA Modules:
  0.0 787.4 jit_solution(1272126847037757994)
XLA Ops:
  7.3 95.2 %all-gather.3.cloned.1.call-done = f32[64,448,128]{2,1,0:T(8,128)} async-done(((f32[2,448,128]{2,1,0:T(8,128)}), f32[64,448,128]{2,1,0:T(8,128)}) %all-gather.3.cloned.1.call-update) | async-done | bytes 14680080 | tf_op jit(solution)/shard_map/all_gather | solution.py:8
  102.6 12.1 %copy.6 = f32[2,32,448,128]{3,2,1,0:T(8,128)} copy(f32[2,32,448,128]{3,2,0,1:T(8,128)} %bitcast.79) | data formatting | bytes 29360128 | tf_op jit(solution)/shard_map/reshape | solution.py:9
  114.6 2.6 constant_dynamic-slice_fusion.1
  118.2 3.4 convolution_bitcast_fusion
  121.7 7.8 fusion.49
  129.5 74.7 %all-reduce.7.cloned.1.call-done = f32[448,128]{1,0:T(8,128)} async-done(((f32[448,128]{1,0:T(8,128)}), f32[448,128]{1,0:T(8,128)}) %all-reduce.7.cloned.1.call-update) | async-done | bytes 229392 | tf_op jit(solution)/shard_map/psum | solution.py:47
  204.1 2.3 convolution_bitcast_fusion.2
  206.7 1.9 slice_bitcast_fusion
  208.6 2.4 copy.9
  211.3 227.3 %all-reduce.13.cloned.1.call-done = (f32[1792,128]{1,0:T(8,128)}, f32[128,128]{0,1:T(8,128)}) async-done(((f32[1792,128]{1,0:T(8,128)}, f32[128,128]{0,1:T(8,128)}), (f32[1792,128]{1,0:T(8,128)}, f32[128,128]{0,1:T(8,128)})) %all-reduce.13.cloned.1.call-update) | async-done | bytes 983056 | tf_op jit(solution)/shard_map/psum | solution.py:33
  438.6 2.2 fusion.31
  440.8 1.1 fusion.35
  443.6 4.9 convolution_subtract_fusion.1
  448.5 3.4 fusion.13
  452.2 7.8 fusion.50
  460.0 76.0 %all-reduce.9.cloned.1.call-done = f32[448,128]{1,0:T(8,128)} async-done(((f32[448,128]{1,0:T(8,128)}), f32[448,128]{1,0:T(8,128)}) %all-reduce.9.cloned.1.call-update) | async-done | bytes 229392 | tf_op jit(solution)/shard_map/psum | solution.py:47
  535.9 2.3 convolution_bitcast_fusion.1
  538.2 2.4 copy.10
  540.6 2.0 fusion.29
  542.6 227.6 %all-reduce.11.cloned.1.call-done = (f32[1792,128]{1,0:T(8,128)}, f32[128,128]{0,1:T(8,128)}) async-done(((f32[1792,128]{1,0:T(8,128)}, f32[128,128]{0,1:T(8,128)}), (f32[1792,128]{1,0:T(8,128)}, f32[128,128]{0,1:T(8,128)})) %all-reduce.11.cloned.1.call-update) | async-done | bytes 983056 | tf_op jit(solution)/shard_map/psum | solution.py:33
  770.2 2.3 fusion.23
  772.5 1.1 fusion.27
  773.9 2.1 fusion
  776.4 4.4 convolution_subtract_fusion
  (40 shorter events, 4.9 us)
Async XLA Ops:
  6.5 96.0 %all-gather.3.cloned.1.call-start = ((), (), s32[]{:S(2)}) async-start(), calls=%async_computation.2 | async-start | bytes 15138816 | tf_op jit(solution)/shard_map/all_gather | solution.py:8
  7.3 196.9 %all-reduce.7.cloned.1.call-start = ((), (), s32[]{:S(2)}) async-start(), calls=%async_computation | async-start | bytes 458752 | tf_op jit(solution)/shard_map/psum | solution.py:47
  114.6 3.6 copy-start
  117.3 0.9 copy-start.2
  121.6 317.0 %all-reduce.13.cloned.1.call-start = ((), (), s32[]{:S(2)}) async-start(), calls=%async_computation.4 | async-start | bytes 1966080 | tf_op jit(solution)/shard_map/psum | solution.py:33
  129.5 81.5 %copy-start.8 = (f32[2,128,128]{2,1,0:T(8,128)S(1)}, f32[2,128,128]{2,1,0:T(8,128)}, u32[]{:S(2)}) copy-start(f32[2,128,128]{2,1,0:T(8,128)} %param.5) | copy-start | bytes 393220
  204.1 6.9 copy-start.10
  206.4 235.8 %copy-start.3 = (f32[1,1792,128]{2,1,0:T(8,128)S(1)}, f32[1,1792,128]{2,1,0:T(8,128)}, u32[]{:S(2)}) copy-start(f32[1,1792,128]{2,1,0:T(8,128)} %copy-done.2) | copy-start | bytes 2752516
  206.5 329.5 %all-reduce.9.cloned.1.call-start = ((), (), s32[]{:S(2)}) async-start(), calls=%async_computation.1 | async-start | bytes 458752 | tf_op jit(solution)/shard_map/psum | solution.py:47
  211.0 232.2 %copy-start.4 = (f32[2,448,128]{2,1,0:T(8,128)S(1)}, f32[2,448,128]{2,1,0:T(8,128)}, u32[]{:S(2)}) copy-start(f32[2,448,128]{2,1,0:T(8,128)} %param.4) | copy-start | bytes 1376260
  438.6 5.0 copy-start.7
  443.6 4.9 copy-start.1
  451.9 318.3 %all-reduce.11.cloned.1.call-start = ((), (), s32[]{:S(2)}) async-start(), calls=%async_computation.3 | async-start | bytes 1966080 | tf_op jit(solution)/shard_map/psum | solution.py:33
  770.2 5.8 copy-start.5
  770.2 5.8 copy-start.11
  770.2 6.2 copy-start.6
  770.2 6.2 copy-start.9
Sparse Core Ops, SparseCore 0:
  9.2 93.3 all-gather.2
  121.7 82.3 all-reduce.6
  206.8 231.7 all-reduce.12
  452.0 83.8 all-reduce.8
  538.5 231.7 all-reduce.10
